TPU v7x, 32 devices: a whole 2x2x4 slice. The times are simulated.
32 devices in a mesh: gx: 4 (over y, x), gz: 4 (over z), gy: 2 (over core).
Axes of the slice: x: 2, y: 2, z: 4, core: 2. Of those that a mesh axis runs over, the one named last changes fastest.
Arguments:
- blocks: bfloat16 [4, 4, 4, 96, 4096], P('gx', 'gz', 'gy'), may hold values from -6 to 6
- block_count: int32 [4, 4, 2], P('gx', 'gz', 'gy'), may hold values from 1 to 2, as said below
- neighbours: int32 [4, 4, 4, 26], P('gx', 'gz', 'gy'), may hold values from -1 to 15, as said below
- conv_weight: bfloat16 [48, 2592], replicated, may hold values from -0.125 to 0.125
- conv_bias: float32 [48], replicated, may hold values from -3 to 3
- head_weight: bfloat16 [48, 48], replicated, may hold values from -0.875 to 0.875
- head_bias: float32 [48], replicated, may hold values from -3 to 3
Outputs:
- features: bfloat16 [4, 4, 4, 48, 4096], P('gx', 'gz', 'gy')
Inputs may be any that keep to these rules, and one draw needn't show every extreme that they name: Each device's foreground blocks fill its first block_count slots; some device fills all 2. `neighbours`: -1 means no foreground block at that offset. Otherwise the value is u + 2 c: used slot u of the device reached from this one by the offset's steps along the axes whose bits are set in c (bit 0 x, bit 1 y, bit 2 z); bits are set only on axes where the offset is nonzero, and c = 0 names this device. Unused slots hold -1 everywhere. Each device's blocks sit at distinct positions of its own region of 2 x 2 x 4 block positions, and the links follow that geometry. The most is reached in every draw.
All inputs are finite; a program needn't handle non-finite values.
Results may differ from a plain program's by a relative error of at most 0.0046.
Values may be sent and summed in bfloat16 or wider, within the bound.
A program may use at most 128 MiB of HBM per device.

v0:
```python
import functools

import jax
import jax.numpy as jnp
import numpy as np
from jax import lax
from jax.experimental import pallas as pl
from jax.experimental.pallas import tpu as pltpu
from jax.sharding import PartitionSpec as P

AXES = ("gx", "gy", "gz")
OFFSETS = [(a, b, c) for a in (-1, 0, 1) for b in (-1, 0, 1) for c in (-1, 0, 1)]
LINKS = [o for o in OFFSETS if o != (0, 0, 0)]
OWN = 27
ZERO = 33


def slot_of(e):
    return (e[0] + 1) * 9 + (e[1] + 1) * 3 + e[2] + 1


def last(step):
    return 0 if step == -1 else 1


def link_tables(slots):
    entry = np.zeros((26, 8), np.int32)
    base = np.zeros((26, 8), np.int32)
    slope = np.zeros((26, 8), np.int32)
    for i, o in enumerate(LINKS):
        for c in range(8):
            if any(c >> a & 1 and o[a] == 0 for a in range(3)):
                continue
            e = tuple(o[a] if c >> a & 1 else 0 for a in range(3))
            if c & 4:
                kind = "z"
            elif c & 1:
                kind = "x"
            elif c & 2:
                kind = "y"
            else:
                kind = "x" if o[0] else "y" if o[1] else "z"
            if c:
                entry[i, c] = slot_of(e) * slots
            else:
                axis = "xyz".index(kind)
                entry[i, c] = (OWN + 2 * axis + last(o[axis])) * slots
            source_x = {-1: 15, 0: 0, 1: 0}[o[0]]
            to_y = 15 if o[1] == 1 else 0
            to_z = 15 if o[2] == 1 else 0
            if kind == "x":
                base[i, c] = 240 * o[1] + 15 * o[2]
            elif kind == "y":
                base[i, c] = (to_y - source_x) * 16 + 15 * o[2]
                slope[i, c] = -16 if o[0] == 0 else 0
            else:
                base[i, c] = 240 * o[1] + to_z - source_x
                slope[i, c] = -1 if o[0] == 0 else 0
    return np.stack([entry, base % 256, slope]).reshape(3, 208)


def exchange_kernel(sizes, slots, blk, pool, send_sem, recv_sem):
    here = {axis: lax.axis_index(axis) for axis in AXES}

    def exists(d):
        ok = None
        for axis, step in zip(AXES, d):
            if step:
                at = here[axis] + step
                good = jnp.logical_and(at >= 0, at < sizes[axis])
                ok = good if ok is None else jnp.logical_and(ok, good)
        return ok

    def target(d):
        return {axis: here[axis] + step for axis, step in zip(AXES, d) if step}

    barrier = pltpu.get_barrier_semaphore()
    greet = 1
    for axis in AXES:
        inner = jnp.where(here[axis] > 0, 1, 0) + jnp.where(here[axis] < sizes[axis] - 1, 1, 0)
        greet = greet * (1 + inner)
    for d in LINKS:
        @pl.when(exists(d))
        def _():
            pl.semaphore_signal(
                barrier, inc=1, device_id=target(d), device_id_type=pl.DeviceIdType.MESH
            )
    pl.semaphore_wait(barrier, greet - 1)

    def copy_of(d):
        e = tuple(-step for step in d)
        at = slot_of(e)
        lanes = slice(0, 256)
        if d[1] and (d[0] or d[2]):
            lanes = slice(128, 256) if d[1] == 1 else slice(0, 128)
        if d[2]:
            src = pool.at[OWN + 4 + last(-d[2]), :, :, lanes]
        elif d[0]:
            start = 15 * 256 if d[0] == 1 else 0
            src = blk.at[:, :, start + lanes.start : start + lanes.stop]
        else:
            src = pool.at[OWN + 2 + last(-d[1])]
        return pltpu.make_async_remote_copy(
            src_ref=src,
            dst_ref=pool.at[at, :, :, lanes],
            send_sem=send_sem.at[at],
            recv_sem=recv_sem.at[at],
            device_id=target(d),
            device_id_type=pl.DeviceIdType.MESH,
        )

    def start(d):
        @pl.when(exists(d))
        def _():
            copy_of(d).start()

    for d in LINKS:
        if d[0] and not d[2]:
            start(d)

    lane = lax.broadcasted_iota(jnp.int32, (blk.shape[1], 128), 1)
    group, place = lane // 16, lane % 16

    def tile(u, x, half):
        at = x * 256 + half * 128
        return blk[u, :, at : at + 128].astype(jnp.float32)

    for side in (0, 1):
        for u in range(slots):
            for half in (0, 1):
                made = None
                for x in range(16):
                    shift = (x - 15) % 128 if side == 0 else x
                    moved = tile(u, x, half)
                    moved = pltpu.roll(moved, shift, 1) if shift else moved
                    made = moved if made is None else jnp.where(place == x, moved, made)
                pool[OWN + 4 + side, u, :, half * 128 : half * 128 + 128] = made.astype(pool.dtype)
    for d in LINKS:
        if d[2]:
            start(d)
    for side in (0, 1):
        for u in range(slots):
            for half in (0, 1):
                made = None
                for k in range(8):
                    x = half * 8 + k
                    shift = (k * 16 - 112) % 128 if side == 0 else k * 16
                    moved = tile(u, x, 1 - side)
                    moved = pltpu.roll(moved, shift, 1) if shift else moved
                    made = moved if made is None else jnp.where(group == k, moved, made)
                pool[OWN + 2 + side, u, :, half * 128 : half * 128 + 128] = made.astype(pool.dtype)
    for d in LINKS:
        if d[1] and not d[0] and not d[2]:
            start(d)
    for u in range(slots):
        pool[OWN, u] = blk[u, :, 15 * 256 : 16 * 256]
        pool[OWN + 1, u] = blk[u, :, 0:256]
        pool[ZERO, u] = jnp.zeros(pool.shape[2:], pool.dtype)
    for d in LINKS:
        @pl.when(exists(d))
        def _():
            copy_of(d).wait_send()
    for d in LINKS:
        e = tuple(-step for step in d)

        @pl.when(exists(e))
        def _():
            copy_of(d).wait_recv()


def conv_kernel(slots, count, links, table, blk, pool, w, cb, hw, hb, out, acc, stack):
    lane = lax.broadcasted_iota(jnp.int32, (blk.shape[1], 256), 1)
    row, col = lane // 16, lane % 16
    channels = blk.shape[1]
    cout = hw.shape[0]

    def roll(value, shift):
        if isinstance(shift, int):
            shift %= 256
            if shift == 0:
                return value
        return pltpu.roll(value, shift, 1)

    def fetch(s, o, x):
        i = LINKS.index(o)
        v = links[s, i]
        c = jnp.maximum(v, 0) // slots
        u = jnp.maximum(v, 0) % slots
        at = i * 8 + c
        entry = jnp.where(v < 0, ZERO * slots, table[0, at] + u)
        shift = lax.rem(table[1, at] + table[2, at] * x + 512, 256)
        return entry, shift

    def piece(s, o, x):
        entry, shift = fetch(s, o, x)
        return roll(pool[entry].astype(jnp.float32), shift)

    def plane(s, p, dx, centre):
        x = p - 1
        rows = {dy: piece(s, (dx, dy, 0), x) for dy in (-1, 1)}

        def put(dy, dz, value):
            t = (dy + 1) * 3 + dz + 1
            stack[t * channels : (t + 1) * channels, :] = value.astype(stack.dtype)

        for dz in (-1, 0, 1):
            if dz == 0:
                mid = centre
            else:
                edge = col == (0 if dz == -1 else 15)
                mid = jnp.where(edge, piece(s, (dx, 0, dz), x), roll(centre, -dz))
            put(0, dz, mid)
            for dy in (-1, 1):
                strip = rows[dy]
                if dz:
                    strip = jnp.where(edge, piece(s, (dx, dy, dz), x), roll(strip, -dz))
                put(dy, dz, jnp.where(row == (0 if dy == -1 else 15), strip, roll(mid, -16 * dy)))
        y = jnp.dot(w[...], stack[...], preferred_element_type=jnp.float32)
        for k in range(3):
            acc[p + 2 - k] += y[k * cout : (k + 1) * cout]

    def per_slot(s, _):
        acc[...] = jnp.zeros_like(acc)
        for p, dx in ((0, -1), (17, 1)):
            entry, _shift = fetch(s, (dx, 0, 0), 0)
            plane(s, p, dx, pool[entry].astype(jnp.float32))

        def inner(p, carry):
            at = pl.multiple_of((p - 1) * 256, 256)
            plane(s, p, 0, blk[s, :, pl.ds(at, 256)].astype(jnp.float32))
            return carry

        lax.fori_loop(1, 17, inner, 0)
        used = s < count[0]

        def finish(x, carry):
            hidden = jnp.maximum(acc[x + 2] + cb[...], 0.0).astype(jnp.bfloat16)
            mixed = jnp.dot(hw[...], hidden, preferred_element_type=jnp.float32) + hb[...]
            mixed = jnp.where(used, mixed, 0.0)
            out[s, :, pl.ds(pl.multiple_of(x * 256, 256), 256)] = mixed.astype(out.dtype)
            return carry

        lax.fori_loop(0, 16, finish, 0)
        return 0

    lax.fori_loop(0, slots, per_slot, 0)


def body(sizes, blocks, block_count, neighbours, conv_weight, conv_bias, head_weight, head_bias):
    slots, channels, voxels = blocks.shape[2:]
    cout = head_weight.shape[0]
    blk = blocks.reshape(slots, channels, voxels)
    vmem = pl.BlockSpec(memory_space=pltpu.VMEM)
    smem = pl.BlockSpec(memory_space=pltpu.SMEM)
    pool = pl.pallas_call(
        functools.partial(exchange_kernel, sizes, slots),
        out_shape=jax.ShapeDtypeStruct((ZERO + 1, slots, channels, 256), blocks.dtype),
        in_specs=[vmem],
        out_specs=vmem,
        scratch_shapes=[pltpu.SemaphoreType.DMA((27,)), pltpu.SemaphoreType.DMA((27,))],
        compiler_params=pltpu.CompilerParams(collective_id=0, has_side_effects=True),
        name="exchange",
    )(blk)
    taps = conv_weight.reshape(cout, 3, 9 * channels).transpose(1, 0, 2).reshape(3 * cout, 9 * channels)
    out = pl.pallas_call(
        functools.partial(conv_kernel, slots),
        out_shape=jax.ShapeDtypeStruct((slots, cout, voxels), jnp.bfloat16),
        in_specs=[smem] * 3 + [vmem] * 6,
        out_specs=vmem,
        scratch_shapes=[
            pltpu.VMEM((20, cout, 256), jnp.float32),
            pltpu.VMEM((9 * channels, 256), jnp.bfloat16),
        ],
        name="conv",
    )(
        block_count.reshape(1),
        neighbours.reshape(slots, 26),
        jnp.asarray(link_tables(slots)),
        blk,
        pool.reshape((ZERO + 1) * slots, channels, 256),
        taps,
        conv_bias[:, None],
        head_weight,
        head_bias[:, None],
    )
    return out.reshape(1, 1, slots, cout, voxels)


def solution(mesh):
    placed = (
        P("gx", "gz", "gy", None, None),
        P("gx", "gz", "gy"),
        P("gx", "gz", "gy", None),
        P(),
        P(),
        P(),
        P(),
    )
    return jax.shard_map(
        functools.partial(body, dict(mesh.shape)),
        mesh=mesh,
        in_specs=placed,
        out_specs=P("gx", "gz", "gy", None, None),
        check_vma=False,
    )
```

profile of v0, /device:TPU:21, one launch (start us, length us, event | category | flops | bytes accessed | tf_op | source)
XLA Modules:
  0.0 63.0 jit_solution(16548046706856766703)
XLA Ops:
  0.7 1.3 %copy.13.cb = f32[48,1]{1,0:T(8,128)} copy(f32[48,1]{0,1:T(1,128)} %bitcast.16) | data formatting | bytes 384 | tf_op jit(solution)/shard_map/broadcast_in_dim | solution.py:282
  2.0 1.3 %copy.14.hb = f32[48,1]{1,0:T(8,128)} copy(f32[48,1]{0,1:T(1,128)} %bitcast.17) | data formatting | bytes 384 | tf_op jit(solution)/shard_map/broadcast_in_dim | solution.py:284
  3.3 1.2 %reshape.25 = bf16[48,3,864]{2,1,0:T(4,128)(2,1)S(1)} reshape(bf16[48,2592]{1,0:T(8,128)(2,1)} %param.11) | data formatting | bytes 497664 | tf_op jit(solution)/shard_map/reshape | solution.py:264
  4.5 0.7 %copy.12 = bf16[3,48,864]{2,1,0:T(8,128)(2,1)} copy(bf16[3,48,864]{2,0,1:T(4,128)(2,1)S(1)} %bitcast.13) | data formatting | bytes 497664 | tf_op jit(solution)/shard_map/transpose | solution.py:264
  5.2 27.4 %exchange.1 = bf16[34,2,96,256]{3,2,1,0:T(8,128)(2,1)} custom-call(bf16[2,96,4096]{2,1,0:T(8,128)(2,1)} %bitcast.11), custom_call_target="tpu_custom_call" | custom-call | tf_op jit(solution)/shard_map/exchange/pallas_call | solution.py:255
  32.7 30.3 %conv.1 = bf16[2,48,4096]{2,1,0:T(8,128)(2,1)} custom-call(s32[1]{0:T(128)} %bitcast.9.count, s32[2,26]{1,0:T(2,128)} %bitcast.15, s32[3,208]{1,0:T(4,128)} %constant.2.clone.table, bf16[2,96,4096]{2,1,0:T(8,128)(2,1)} %bitcast.12, bf16[68,96,256]{2,1,0:T(8,128)(2,1)} %bitcast.10, bf16[144,864]{1,0:T(8,128)(2,1)} %bitcast.14, f32[48,1]{1,0:T(8,128)} %copy.13.cb, ...), custom_call_target="tpu_custom_call" | custom-call | tf_op jit(solution)/shard_map/conv/pallas_call | solution.py:265
where the time goes:
time: 63.2 us; the launch traced here: 63 us
  Pallas kernels  57.7 us (91%)
  local copies, waits for them, and re-layouts  4.58 us (7%)
  between operations  0.67 us (1%)
    pallas_call x1, Pallas kernels, body(): pl.pallas_call(functools.partial(conv_kernel, slots), out_shape=jax.Shape...  30.3 us
    pallas_call x1, Pallas kernels, body(): pl.pallas_call(functools.partial(exchange_kernel, sizes, slots), out_shap...  27.4 us
    broadcast_in_dim x1, local copies, waits for them, and re-layouts, body(): head_bias[:, None]  1.34 us
    broadcast_in_dim x1, local copies, waits for them, and re-layouts, body(): conv_bias[:, None]  1.34 us

commit v1 on v0

v1 whole, which is shorter than its diff:
```python
import functools

import jax
import jax.numpy as jnp
import numpy as np
from jax import lax
from jax.experimental import pallas as pl
from jax.experimental.pallas import tpu as pltpu
from jax.sharding import PartitionSpec as P

AXES = ("gx", "gy", "gz")
OFFSETS = [(a, b, c) for a in (-1, 0, 1) for b in (-1, 0, 1) for c in (-1, 0, 1)]
LINKS = [o for o in OFFSETS if o != (0, 0, 0)]
OWN = 27
ZERO = 33


def slot_of(e):
    return (e[0] + 1) * 9 + (e[1] + 1) * 3 + e[2] + 1


def last(step):
    return 0 if step == -1 else 1


def link_tables(slots):
    entry = np.zeros((26, 8), np.int32)
    base = np.zeros((26, 8), np.int32)
    slope = np.zeros((26, 8), np.int32)
    for i, o in enumerate(LINKS):
        for c in range(8):
            if any(c >> a & 1 and o[a] == 0 for a in range(3)):
                continue
            e = tuple(o[a] if c >> a & 1 else 0 for a in range(3))
            if c & 4:
                kind = "z"
            elif c & 1:
                kind = "x"
            elif c & 2:
                kind = "y"
            else:
                kind = "x" if o[0] else "y" if o[1] else "z"
            if c:
                entry[i, c] = slot_of(e) * slots
            else:
                axis = "xyz".index(kind)
                entry[i, c] = (OWN + 2 * axis + last(o[axis])) * slots
            source_x = {-1: 15, 0: 0, 1: 0}[o[0]]
            to_y = 15 if o[1] == 1 else 0
            to_z = 15 if o[2] == 1 else 0
            if kind == "x":
                base[i, c] = 240 * o[1] + 15 * o[2]
            elif kind == "y":
                base[i, c] = (to_y - source_x) * 16 + 15 * o[2]
                slope[i, c] = -16 if o[0] == 0 else 0
            else:
                base[i, c] = 240 * o[1] + to_z - source_x
                slope[i, c] = -1 if o[0] == 0 else 0
    return np.stack([entry, base % 256, slope]).reshape(3, 208)


def exchange_kernel(sizes, slots, blk, pool, gone, came, send_sem, recv_sem):
    here = {axis: lax.axis_index(axis) for axis in AXES}

    def exists(d):
        ok = None
        for axis, step in zip(AXES, d):
            if step:
                at = here[axis] + step
                good = jnp.logical_and(at >= 0, at < sizes[axis])
                ok = good if ok is None else jnp.logical_and(ok, good)
        return ok

    def target(d):
        return {axis: here[axis] + step for axis, step in zip(AXES, d) if step}

    barrier = pltpu.get_barrier_semaphore()
    greet = 1
    for axis in AXES:
        inner = jnp.where(here[axis] > 0, 1, 0) + jnp.where(here[axis] < sizes[axis] - 1, 1, 0)
        greet = greet * (1 + inner)
    for d in LINKS:
        @pl.when(exists(d))
        def _():
            pl.semaphore_signal(
                barrier, inc=1, device_id=target(d), device_id_type=pl.DeviceIdType.MESH
            )
    pl.semaphore_wait(barrier, greet - 1)

    lane = lax.broadcasted_iota(jnp.int32, (blk.shape[1], 128), 1)
    group, place = lane // 16, lane % 16

    def roll(value, shift):
        shift %= 128
        return pltpu.roll(value, shift, 1) if shift else value

    def end_lanes(step):
        return slice(128, 256) if step == 1 else slice(0, 128)

    def packed(d):
        if d[1] and d[2]:
            return 8 + (d[1] + 1) + (d[2] + 1) // 2
        if d[1]:
            return (d[0] + 1) + (d[1] + 1) // 2
        return 4 + (d[0] + 1) + (d[2] + 1) // 2

    def copy_of(d):
        at = slot_of(tuple(-step for step in d))
        dst = pool.at[at]
        if sum(map(abs, d)) > 1:
            src, dst = gone.at[packed(d)], came.at[at]
        elif d[0]:
            src = blk.at[:, :, (15 * 256 if d[0] == 1 else 0) : (16 * 256 if d[0] == 1 else 256)]
        else:
            src = pool.at[OWN + (2 if d[1] else 4) + last(-d[1] - d[2])]
        return pltpu.make_async_remote_copy(
            src_ref=src,
            dst_ref=dst,
            send_sem=send_sem.at[at],
            recv_sem=recv_sem.at[at],
            device_id=target(d),
            device_id_type=pl.DeviceIdType.MESH,
        )

    def start(d):
        @pl.when(exists(d))
        def _():
            copy_of(d).start()

    def end_row(d, first, second):
        keep = group == (7 if d[1] == 1 else 0)
        return jnp.where(keep, first, roll(second, 64))

    start((1, 0, 0))
    start((-1, 0, 0))

    def tile(u, x, half):
        at = x * 256 + half * 128
        return blk[u, :, at : at + 128]

    for d in LINKS:
        if d[0] and d[1] and not d[2]:
            x, half = (15 if d[0] == 1 else 0), (1 if d[1] == 1 else 0)
            gone[packed(d)] = end_row(d, tile(0, x, half), tile(1, x, half))
            start(d)
    for dz in (1, -1):
        side = last(-dz)
        faces = {}
        for u in range(slots):
            for half in (0, 1):
                made = None
                for x in range(16):
                    moved = roll(tile(u, x, half), x - 15 if side == 0 else x)
                    made = moved if made is None else jnp.where(place == x, moved, made)
                pool[OWN + 4 + side, u, :, half * 128 : half * 128 + 128] = made
                faces[u, half] = made
        start((0, 0, dz))
        for dx in (1, -1):
            d = (dx, 0, dz)
            made = None
            for u in range(slots):
                for half in (0, 1):
                    moved = roll(faces[u, half], 2 * u + half - (15 if dx == 1 else 0))
                    made = moved if made is None else jnp.where(place == 2 * u + half, moved, made)
            gone[packed(d)] = made
            start(d)
        for dy in (1, -1):
            d = (0, dy, dz)
            half = 1 if dy == 1 else 0
            gone[packed(d)] = end_row(d, faces[0, half], faces[1, half])
            for dx in (0, 1, -1):
                start((dx, dy, dz))
    for side in (0, 1):
        for u in range(slots):
            for half in (0, 1):
                made = None
                for k in range(8):
                    moved = roll(tile(u, half * 8 + k, 1 - side), k * 16 - (112 if side == 0 else 0))
                    made = moved if made is None else jnp.where(group == k, moved, made)
                pool[OWN + 2 + side, u, :, half * 128 : half * 128 + 128] = made
        start((0, 1 if side == 0 else -1, 0))
    for u in range(slots):
        pool[OWN, u] = blk[u, :, 15 * 256 : 16 * 256]
        pool[OWN + 1, u] = blk[u, :, 0:256]
        pool[ZERO, u] = jnp.zeros(pool.shape[2:], pool.dtype)
    for d in LINKS:
        e = tuple(-step for step in d)
        at = slot_of(e)

        @pl.when(exists(e))
        def _():
            copy_of(d).wait_recv()
            if sum(map(abs, d)) == 1:
                return
            message = came[at]
            if d[1]:
                for u in range(slots):
                    pool[at, u, :, end_lanes(d[1])] = roll(message, 64 * u)
            else:
                for u in range(slots):
                    for half in (0, 1):
                        back = (15 if d[0] == 1 else 0) - 2 * u - half
                        pool[at, u, :, half * 128 : half * 128 + 128] = roll(message, back)
    for d in LINKS:
        @pl.when(exists(d))
        def _():
            copy_of(d).wait_send()


def conv_kernel(slots, count, links, table, blk, pool, cw, cb, hw, hb, out, w, acc, even, odd):
    channels = blk.shape[1]
    cout = hw.shape[0]
    lane = lax.broadcasted_iota(jnp.int32, (channels, 256), 1)
    row, col = lane // 16, lane % 16
    eye = lax.broadcasted_iota(jnp.int32, (cout, cout), 0) == lax.broadcasted_iota(
        jnp.int32, (cout, cout), 1
    )

    def column(ref):
        return jnp.sum(jnp.where(eye, ref[...], 0.0), axis=1, keepdims=True)

    bias, head_bias = column(cb), column(hb)
    depth = 9 * channels
    for k in range(3):
        w[k * cout : (k + 1) * cout, :] = cw[:, k * depth : (k + 1) * depth]

    def fetch(s, o, x):
        i = LINKS.index(o)
        v = links[s, i]
        c = jnp.maximum(v, 0) // slots
        u = jnp.maximum(v, 0) % slots
        at = i * 8 + c
        entry = jnp.where(v < 0, ZERO * slots, table[0, at] + u)
        shift = lax.rem(table[1, at] + table[2, at] * x + 512, 256)
        return entry, shift

    def part(s, o, x):
        entry, shift = fetch(s, o, x)
        lands = (15 if o[1] == 1 else 0) * 16 + (15 if o[2] == 1 else 0)
        half = lax.rem(lands - shift + 256, 256) // 128
        got = pool[entry, :, pl.ds(pl.multiple_of(half * 128, 128), 128)]
        return pltpu.roll(got, lax.rem(shift, 128), 1)

    def build(stack, s, p, dx, centre):
        x = p - 1
        rows = {dy: part(s, (dx, dy, 0), x) for dy in (-1, 1)}
        for dz in (-1, 0, 1):
            mid = centre
            if dz:
                edge = col == (0 if dz == -1 else 15)
                entry, shift = fetch(s, (dx, 0, dz), x)
                mid = jnp.where(edge, pltpu.roll(pool[entry], shift, 1), pltpu.roll(centre, -dz % 256, 1))
            for dy in (-1, 0, 1):
                t = ((dy + 1) * 3 + dz + 1) * channels
                if dy == 0:
                    stack[t : t + channels, :] = mid
                    continue
                moved = pltpu.roll(mid, -16 * dy % 256, 1)
                strip = rows[dy]
                lanes = slice(0, 128) if dy == -1 else slice(128, 256)
                if dz:
                    strip = jnp.where(
                        edge[:, lanes], part(s, (dx, dy, dz), x), pltpu.roll(strip, -dz % 128, 1)
                    )
                other = slice(128, 256) if dy == -1 else slice(0, 128)
                stack[t : t + channels, other] = moved[:, other]
                stack[t : t + channels, lanes] = jnp.where(
                    row[:, lanes] == (0 if dy == -1 else 15), strip, moved[:, lanes]
                )

    def multiply(stack, p):
        y = jnp.dot(w[...], stack[...], preferred_element_type=jnp.float32)
        for k in range(3):
            acc[p + 2 - k] += y[k * cout : (k + 1) * cout]

    def per_slot(s, _):
        acc[...] = jnp.zeros_like(acc)

        def shell(stack, p, dx):
            entry, _shift = fetch(s, (dx, 0, 0), 0)
            build(stack, s, p, dx, pool[entry])

        def inside(stack, p):
            at = pl.multiple_of((p - 1) * 256, 256)
            build(stack, s, p, 0, blk[s, :, pl.ds(at, 256)])

        shell(even, 0, -1)

        def inner(k, carry):
            inside(odd, 2 * k + 1)
            multiply(even, 2 * k)
            inside(even, 2 * k + 2)
            multiply(odd, 2 * k + 1)
            return carry

        lax.fori_loop(0, 8, inner, 0)
        shell(odd, 17, 1)
        multiply(even, 16)
        multiply(odd, 17)
        used = s < count[0]

        def finish(x, carry):
            hidden = jnp.maximum(acc[x + 2] + bias, 0.0).astype(jnp.bfloat16)
            mixed = jnp.dot(hw[...], hidden, preferred_element_type=jnp.float32) + head_bias
            mixed = jnp.where(used, mixed, 0.0)
            out[s, :, pl.ds(pl.multiple_of(x * 256, 256), 256)] = mixed.astype(out.dtype)
            return carry

        lax.fori_loop(0, 16, finish, 0, unroll=4)
        return 0

    lax.fori_loop(0, slots, per_slot, 0)


def body(sizes, blocks, block_count, neighbours, conv_weight, conv_bias, head_weight, head_bias):
    slots, channels, voxels = blocks.shape[2:]
    cout = head_weight.shape[0]
    blk = blocks.reshape(slots, channels, voxels)
    vmem = pl.BlockSpec(memory_space=pltpu.VMEM)
    smem = pl.BlockSpec(memory_space=pltpu.SMEM)
    pool = pl.pallas_call(
        functools.partial(exchange_kernel, sizes, slots),
        out_shape=jax.ShapeDtypeStruct((ZERO + 1, slots, channels, 256), blocks.dtype),
        in_specs=[vmem],
        out_specs=vmem,
        scratch_shapes=[
            pltpu.VMEM((12, channels, 128), blocks.dtype),
            pltpu.VMEM((27, channels, 128), blocks.dtype),
            pltpu.SemaphoreType.DMA((27,)),
            pltpu.SemaphoreType.DMA((27,)),
        ],
        compiler_params=pltpu.CompilerParams(collective_id=0, has_side_effects=True),
        name="exchange",
    )(blk)
    out = pl.pallas_call(
        functools.partial(conv_kernel, slots),
        out_shape=jax.ShapeDtypeStruct((slots, cout, voxels), jnp.bfloat16),
        in_specs=[smem] * 3 + [vmem] * 6,
        out_specs=vmem,
        scratch_shapes=[
            pltpu.VMEM((3 * cout, 9 * channels), jnp.bfloat16),
            pltpu.VMEM((20, cout, 256), jnp.float32),
            pltpu.VMEM((9 * channels, 256), jnp.bfloat16),
            pltpu.VMEM((9 * channels, 256), jnp.bfloat16),
        ],
        name="conv",
    )(
        block_count.reshape(1),
        neighbours.reshape(slots, 26),
        jnp.asarray(link_tables(slots)),
        blk,
        pool.reshape((ZERO + 1) * slots, channels, 256),
        conv_weight,
        conv_bias[None],
        head_weight,
        head_bias[None],
    )
    return out.reshape(1, 1, slots, cout, voxels)


def solution(mesh):
    placed = (
        P("gx", "gz", "gy", None, None),
        P("gx", "gz", "gy"),
        P("gx", "gz", "gy", None),
        P(),
        P(),
        P(),
        P(),
    )
    return jax.shard_map(
        functools.partial(body, dict(mesh.shape)),
        mesh=mesh,
        in_specs=placed,
        out_specs=P("gx", "gz", "gy", None, None),
        check_vma=False,
    )
```

time: 63.2 us -> 37.1 us (0.59)
  Pallas kernels: 57.7 us -> 35.8 us
  local copies, waits for them, and re-layouts: 4.58 us -> 0 us
    pallas_call x1, Pallas kernels: 30.3 us -> 17.7 us  [body(): pl.pallas_call(functools.partial(conv_kernel, slots), out_shape=jax.Shape...]
    pallas_call x1, Pallas kernels: 27.4 us -> 18.2 us  [body(): pl.pallas_call(functools.partial(exchange_kernel, sizes, slots), out_shap...]
    broadcast_in_dim x2 -> x0, local copies, waits for them, and re-layouts: 2.68 us -> none  [the longest x1 1.34 us: body(): head_bias[:, None]]
    reshape x1 -> x0, local copies, waits for them, and re-layouts: 1.16 us -> none  [body(): conv_weight.reshape(cout, 3, 9 * channels).transpose(1, 0, 2)]
    transpose x1 -> x0, local copies, waits for them, and re-layouts: 0.74 us -> none  [body(): conv_weight.reshape(cout, 3, 9 * channels).transpose(1, 0, 2)]
where the time goes in v1:
time: 37.1 us; the launch traced here: 36.5 us
  Pallas kernels  35.8 us (96%)
  between operations  0.66 us (2%)
    pallas_call x1, Pallas kernels, body(): pl.pallas_call(functools.partial(exchange_kernel, sizes, slots), out_shap...  18.2 us
    pallas_call x1, Pallas kernels, body(): pl.pallas_call(functools.partial(conv_kernel, slots), out_shape=jax.Shape...  17.7 us

profile of v1, /device:TPU:21, one launch (start us, length us, event | category | flops | bytes accessed | tf_op | source)
XLA Modules:
  0.0 36.5 jit_solution(12793436496012014394)
XLA Ops:
  0.7 18.2 %exchange.1 = bf16[34,2,96,256]{3,2,1,0:T(8,128)(2,1)} custom-call(bf16[2,96,4096]{2,1,0:T(8,128)(2,1)} %bitcast.9), custom_call_target="tpu_custom_call" | custom-call | tf_op jit(solution)/shard_map/exchange/pallas_call | solution.py:321
  18.8 17.7 %conv.1 = bf16[2,48,4096]{2,1,0:T(8,128)(2,1)} custom-call(s32[1]{0:T(128)} %bitcast.7.count, s32[2,26]{1,0:T(2,128)} %bitcast.11, s32[3,208]{1,0:T(4,128)} %constant.2.clone.table, bf16[2,96,4096]{2,1,0:T(8,128)(2,1)} %bitcast.10, bf16[68,96,256]{2,1,0:T(8,128)(2,1)} %bitcast.8, bf16[48,2592]{1,0:T(8,128)(2,1)} %cw.1, f32[1,48]{1,0:T(1,128)} %bitcast.12, ...), custom_call_target="tpu_custom_call" | custom-call | tf_op jit(solution)/shard_map/conv/pallas_call | solution.py:335

commit v2 on v1

--- a/solution.py
+++ b/solution.py
@@ -85,8 +85,6 @@
             pl.semaphore_signal(
                 barrier, inc=1, device_id=target(d), device_id_type=pl.DeviceIdType.MESH
             )
-    pl.semaphore_wait(barrier, greet - 1)
-
     lane = lax.broadcasted_iota(jnp.int32, (blk.shape[1], 128), 1)
     group, place = lane // 16, lane % 16
 
@@ -131,9 +129,6 @@
         keep = group == (7 if d[1] == 1 else 0)
         return jnp.where(keep, first, roll(second, 64))
 
-    start((1, 0, 0))
-    start((-1, 0, 0))
-
     def tile(u, x, half):
         at = x * 256 + half * 128
         return blk[u, :, at : at + 128]
@@ -142,7 +137,6 @@
         if d[0] and d[1] and not d[2]:
             x, half = (15 if d[0] == 1 else 0), (1 if d[1] == 1 else 0)
             gone[packed(d)] = end_row(d, tile(0, x, half), tile(1, x, half))
-            start(d)
     for dz in (1, -1):
         side = last(-dz)
         faces = {}
@@ -154,7 +148,6 @@
                     made = moved if made is None else jnp.where(place == x, moved, made)
                 pool[OWN + 4 + side, u, :, half * 128 : half * 128 + 128] = made
                 faces[u, half] = made
-        start((0, 0, dz))
         for dx in (1, -1):
             d = (dx, 0, dz)
             made = None
@@ -163,13 +156,10 @@
                     moved = roll(faces[u, half], 2 * u + half - (15 if dx == 1 else 0))
                     made = moved if made is None else jnp.where(place == 2 * u + half, moved, made)
             gone[packed(d)] = made
-            start(d)
         for dy in (1, -1):
             d = (0, dy, dz)
             half = 1 if dy == 1 else 0
             gone[packed(d)] = end_row(d, faces[0, half], faces[1, half])
-            for dx in (0, 1, -1):
-                start((dx, dy, dz))
     for side in (0, 1):
         for u in range(slots):
             for half in (0, 1):
@@ -178,7 +168,9 @@
                     moved = roll(tile(u, half * 8 + k, 1 - side), k * 16 - (112 if side == 0 else 0))
                     made = moved if made is None else jnp.where(group == k, moved, made)
                 pool[OWN + 2 + side, u, :, half * 128 : half * 128 + 128] = made
-        start((0, 1 if side == 0 else -1, 0))
+    pl.semaphore_wait(barrier, greet - 1)
+    for d in sorted(LINKS, key=lambda d: (sum(map(abs, d)), -abs(d[0]))):
+        start(d)
     for u in range(slots):
         pool[OWN, u] = blk[u, :, 15 * 256 : 16 * 256]
         pool[OWN + 1, u] = blk[u, :, 0:256]

time: 37.1 us -> 37 us (level)
  no operation moved by 1% of the time
where the time goes in v2:
time: 37 us; the launch traced here: 36.5 us
  Pallas kernels  35.8 us (97%)
  between operations  0.66 us (2%)
    pallas_call x1, Pallas kernels, body(): pl.pallas_call(functools.partial(exchange_kernel, sizes, slots), out_shap...  18.2 us
    pallas_call x1, Pallas kernels, body(): pl.pallas_call(functools.partial(conv_kernel, slots), out_shape=jax.Shape...  17.7 us

profile of v2, /device:TPU:21, one launch (start us, length us, event | category | flops | bytes accessed | tf_op | source)
XLA Modules:
  0.0 36.5 jit_solution(11243157330009883239)
XLA Ops:
  0.7 18.2 %exchange.1 = bf16[34,2,96,256]{3,2,1,0:T(8,128)(2,1)} custom-call(bf16[2,96,4096]{2,1,0:T(8,128)(2,1)} %bitcast.9), custom_call_target="tpu_custom_call" | custom-call | tf_op jit(solution)/shard_map/exchange/pallas_call | solution.py:313
  18.8 17.7 %conv.1 = bf16[2,48,4096]{2,1,0:T(8,128)(2,1)} custom-call(s32[1]{0:T(128)} %bitcast.7.count, s32[2,26]{1,0:T(2,128)} %bitcast.11, s32[3,208]{1,0:T(4,128)} %constant.2.clone.table, bf16[2,96,4096]{2,1,0:T(8,128)(2,1)} %bitcast.10, bf16[68,96,256]{2,1,0:T(8,128)(2,1)} %bitcast.8, bf16[48,2592]{1,0:T(8,128)(2,1)} %cw.1, f32[1,48]{1,0:T(1,128)} %bitcast.12, ...), custom_call_target="tpu_custom_call" | custom-call | tf_op jit(solution)/shard_map/conv/pallas_call | solution.py:327

commit v3 on v2

--- a/solution.py
+++ b/solution.py
@@ -321,7 +321,7 @@
             pltpu.SemaphoreType.DMA((27,)),
             pltpu.SemaphoreType.DMA((27,)),
         ],
-        compiler_params=pltpu.CompilerParams(collective_id=0, has_side_effects=True),
+        compiler_params=pltpu.CompilerParams(collective_id=0, has_side_effects=True, vmem_limit_bytes=16 << 20),
         name="exchange",
     )(blk)
     out = pl.pallas_call(
@@ -335,6 +335,7 @@
             pltpu.VMEM((9 * channels, 256), jnp.bfloat16),
             pltpu.VMEM((9 * channels, 256), jnp.bfloat16),
         ],
+        compiler_params=pltpu.CompilerParams(vmem_limit_bytes=20 << 20),
         name="conv",
     )(
         block_count.reshape(1),

time: 37 us -> 33.7 us (0.911)
  Pallas kernels: 35.8 us -> 30.9 us
  local copies, waits for them, and re-layouts: 0 us -> 1.43 us
    pallas_call x1, Pallas kernels: 18.2 us -> 15.1 us  [body(): pl.pallas_call(functools.partial(exchange_kernel, sizes, slots), out_shap...]
    pallas_call x1, Pallas kernels: 17.7 us -> 15.8 us  [body(): pl.pallas_call(functools.partial(conv_kernel, slots), out_shape=jax.Shape...]
    unnamed x0 -> x16, local copies, waits for them, and re-layouts: none -> 1.43 us
where the time goes in v3:
time: 33.7 us; the launch traced here: 33.1 us
  Pallas kernels  30.9 us (92%)
  local copies, waits for them, and re-layouts  1.43 us (4%)
  between operations  0.78 us (2%)
    pallas_call x1, Pallas kernels, body(): pl.pallas_call(functools.partial(conv_kernel, slots), out_shape=jax.Shape...  15.8 us
    pallas_call x1, Pallas kernels, body(): pl.pallas_call(functools.partial(exchange_kernel, sizes, slots), out_shap...  15.1 us
    unnamed x16, local copies, waits for them, and re-layouts  1.43 us

profile of v3, /device:TPU:21, one launch (start us, length us, event | category | flops | bytes accessed | tf_op | source)
XLA Modules:
  0.0 33.1 jit_solution(13314410695227398628)
XLA Ops:
  0.0 0.0 copy-start.4
  0.0 0.0 copy-start.7
  0.0 0.0 copy-start.6
  0.0 0.0 copy-start.5
  0.7 0.0 copy-start
  0.7 1.4 %copy-done = bf16[1,1,2,96,4096]{4,3,2,1,0:T(8,128)(2,1)S(1)} copy-done((bf16[1,1,2,96,4096]{4,3,2,1,0:T(8,128)(2,1)S(1)}, bf16[1,1,2,96,4096]{4,3,2,1,0:T(8,128)(2,1)}, u32[]{:S(2)}) %copy-start) | copy-done | bytes 1572888
  2.1 0.0 copy-start.1
  2.1 0.0 copy-start.2
  2.1 0.0 copy-start.3
  2.1 15.1 %exchange.1 = bf16[34,2,96,256]{3,2,1,0:T(8,128)(2,1)S(1)} custom-call(bf16[2,96,4096]{2,1,0:T(8,128)(2,1)S(1)} %bitcast.9), custom_call_target="tpu_custom_call" | custom-call | tf_op jit(solution)/shard_map/exchange/pallas_call | solution.py:313
  17.2 0.0 copy-done.4
  17.2 0.0 copy-done.7
  17.2 0.0 copy-done.6
  17.2 0.0 copy-done.5
  17.2 0.0 copy-done.1
  17.3 0.0 copy-done.2
  17.3 0.0 copy-done.3
  17.3 15.8 %conv.1 = bf16[2,48,4096]{2,1,0:T(8,128)(2,1)} custom-call(s32[1]{0:T(128)} %bitcast.7.count, s32[2,26]{1,0:T(2,128)S(1)} %bitcast.11, s32[3,208]{1,0:T(4,128)S(1)} %copy-done.4, bf16[2,96,4096]{2,1,0:T(8,128)(2,1)S(1)} %bitcast.10, bf16[68,96,256]{2,1,0:T(8,128)(2,1)S(1)} %bitcast.8, bf16[48,2592]{1,0:T(8,128)(2,1)S(1)} %copy-done.2, f32[1,48]{1,0:T(1,128)S(1)} %bitcast.12, ...), custom_call_target="tpu_custom_call" | custom-call | tf_op jit(solution)/shard_map/conv/pallas_call | solution.py:327
Async XLA Ops:
  0.0 17.2 %copy-start.4 = (s32[3,208]{1,0:T(4,128)S(1)}, s32[3,208]{1,0:T(4,128)}, u32[]{:S(2)}) copy-start(s32[3,208]{1,0:T(4,128)} %constant.2.clone.table) | copy-start | bytes 7492
  0.0 17.2 %copy-start.7 = (f32[48]{0:T(128)S(1)}, f32[48]{0:T(128)}, u32[]{:S(2)}) copy-start(f32[48]{0:T(128)} %param.14) | copy-start | bytes 580
  0.0 17.2 %copy-start.6 = (f32[48]{0:T(128)S(1)}, f32[48]{0:T(128)}, u32[]{:S(2)}) copy-start(f32[48]{0:T(128)} %param.12) | copy-start | bytes 580
  0.0 17.2 %copy-start.5 = (s32[1,1,2,26]{3,2,1,0:T(2,128)S(1)}, s32[1,1,2,26]{3,2,1,0:T(2,128)}, u32[]{:S(2)}) copy-start(s32[1,1,2,26]{3,2,1,0:T(2,128)} %param.10) | copy-start | bytes 628
  0.7 1.4 %copy-start = (bf16[1,1,2,96,4096]{4,3,2,1,0:T(8,128)(2,1)S(1)}, bf16[1,1,2,96,4096]{4,3,2,1,0:T(8,128)(2,1)}, u32[]{:S(2)}) copy-start(bf16[1,1,2,96,4096]{4,3,2,1,0:T(8,128)(2,1)} %param.8) | copy-start | bytes 4718596
  2.1 15.1 %copy-start.1 = (bf16[1,1,2,96,4096]{4,3,2,1,0:T(8,128)(2,1)S(1)}, bf16[1,1,2,96,4096]{4,3,2,1,0:T(8,128)(2,1)}, u32[]{:S(2)}) copy-start(bf16[1,1,2,96,4096]{4,3,2,1,0:T(8,128)(2,1)} %param.8) | copy-start | bytes 4718596
  2.1 15.1 %copy-start.2 = (bf16[48,2592]{1,0:T(8,128)(2,1)S(1)}, bf16[48,2592]{1,0:T(8,128)(2,1)}, u32[]{:S(2)}) copy-start(bf16[48,2592]{1,0:T(8,128)(2,1)} %cw.1) | copy-start | bytes 746500
  2.1 15.1 %copy-start.3 = (bf16[48,48]{1,0:T(8,128)(2,1)S(1)}, bf16[48,48]{1,0:T(8,128)(2,1)}, u32[]{:S(2)}) copy-start(bf16[48,48]{1,0:T(8,128)(2,1)} %hw.1) | copy-start | bytes 13828
